TPU v7x, 256 devices: a whole 4x4x8 slice. The times are simulated.
256 devices in a mesh: grp: 4 (over y_lo, core), trk: 64 (over z, x, y_hi).
Axes of the slice: x: 4, y: 4 (y_hi: 2, y_lo: 2; y = y_hi * 2 + y_lo), z: 8, core: 2. Of those that a mesh axis runs over, the one named last changes fastest.
Arguments:
- fields: bfloat16 [256, 512, 512], P('grp', 'trk'), may hold values from -81 to 81
- upstream: bfloat16 [256, 512, 512], P('grp', 'trk'), may hold values from -6 to 6
- ln_gain: float32 [512], replicated, may hold values from 0.1 to 1.9
- weights: bfloat16 [4, 512, 512], P(None, 'grp', 'trk'), may hold values from -8 to 8
Outputs:
- grad_fields: bfloat16 [256, 512, 512], P('grp', 'trk')
- grad_weights: float32 [4, 512, 512], P(None, 'grp', 'trk')
- grad_gain: float32 [512], replicated
All inputs are finite; a program needn't handle non-finite values.
Results may differ from a plain program's by a relative error of at most 0.014.
The roundings to bfloat16 on the way count: a program that leaves them out, or rounds other values in their place, can miss the bound.
Values may be sent and summed in bfloat16 or wider, within the bound.
A program may use at most 64 MiB of HBM per device.

v0:
```python
import jax
import jax.numpy as jnp
from jax import lax
from jax.sharding import PartitionSpec as P

HEADS = 8


def normalize(fields, ln_gain):
    values = fields.astype(jnp.float32)
    row_mean = jnp.mean(values, -1, keepdims=True)
    offset = values - row_mean
    row_var = jnp.mean(offset * offset, -1, keepdims=True)
    inv_std = lax.rsqrt(row_var + 1e-05)
    centred = offset * inv_std
    normed = (centred * ln_gain).astype(jnp.bfloat16)
    return (normed, centred, inv_std)


def project(normed, w_in):
    return [
        jnp.einsum("rti,ij->rtj", normed, w_in[index], preferred_element_type=jnp.float32).astype(
            jnp.bfloat16
        )
        for index in range(3)
    ]


def split_heads(block, heads):
    rows, length, width = block.shape
    return (
        block.reshape(rows, length, heads, width // heads)
        .transpose(0, 2, 1, 3)
        .reshape(rows * heads, length, width // heads)
    )


def merge_heads(block, rows):
    items, length, size = block.shape
    return (
        block.reshape(rows, items // rows, length, size)
        .transpose(0, 2, 1, 3)
        .reshape(rows, length, items // rows * size)
    )


def head_back(members):
    query, keyed, valued, grad_out = members
    scaling = query.shape[-1] ** (-0.5)
    scores = jnp.einsum("qd,kd->qk", query, keyed, preferred_element_type=jnp.float32) * scaling
    row_max = jnp.max(scores, -1, keepdims=True)
    shifted = jnp.exp(scores - row_max)
    attn_prob = shifted / jnp.sum(shifted, -1, keepdims=True)
    prob_low = attn_prob.astype(jnp.bfloat16)
    output = jnp.einsum("qk,kd->qd", prob_low, valued, preferred_element_type=jnp.float32).astype(
        jnp.bfloat16
    )
    dprobs = jnp.einsum("qd,kd->qk", grad_out, valued, preferred_element_type=jnp.float32)
    row_dot = jnp.sum(attn_prob * dprobs, -1, keepdims=True)
    score_grad = (attn_prob * (dprobs - row_dot) * scaling).astype(jnp.bfloat16)
    grad_value = jnp.einsum(
        "qk,qd->kd", prob_low, grad_out, preferred_element_type=jnp.float32
    ).astype(jnp.bfloat16)
    grad_query = jnp.einsum(
        "qk,kd->qd", score_grad, keyed, preferred_element_type=jnp.float32
    ).astype(jnp.bfloat16)
    grad_key = jnp.einsum(
        "qk,qd->kd", score_grad, query, preferred_element_type=jnp.float32
    ).astype(jnp.bfloat16)
    return (output, grad_query, grad_key, grad_value)


def attend_back(query_proj, key_proj, value_proj, upstream_rows, w_out):
    rows = query_proj.shape[0]
    grad_attended = jnp.einsum(
        "rtj,ij->rti", upstream_rows, w_out, preferred_element_type=jnp.float32
    ).astype(jnp.bfloat16)
    pieces = lax.map(
        head_back,
        (
            split_heads(query_proj, HEADS),
            split_heads(key_proj, HEADS),
            split_heads(value_proj, HEADS),
            split_heads(grad_attended, HEADS),
        ),
    )
    return [merge_heads(piece, rows) for piece in pieces]


def input_grad(grad_query, grad_key, grad_value, w_in, centred, inv_std, ln_gain):
    stacked = jnp.stack([grad_query, grad_key, grad_value], 2)
    grad_normed = jnp.einsum("rtcj,cij->rti", stacked, w_in, preferred_element_type=jnp.float32)
    width = grad_normed.shape[-1]
    gain_term = jnp.sum((grad_normed * centred).reshape(-1, width), 0)
    scaled = grad_normed * ln_gain
    branch = inv_std * (
        scaled
        - jnp.mean(scaled, -1, keepdims=True)
        - centred * jnp.mean(scaled * centred, -1, keepdims=True)
    )
    return (branch.astype(jnp.bfloat16), gain_term)


def proj_grads(normed, grad_query, grad_key, grad_value):
    return [
        jnp.einsum("rti,rtj->ij", normed, member, preferred_element_type=jnp.float32)
        for member in (grad_query, grad_key, grad_value)
    ]


def shards(fields, upstream, ln_gain, weights):
    w_part = lax.all_gather(weights, "trk", axis=2, tiled=True)
    w_full = lax.all_gather(w_part, "grp", axis=1, tiled=True)
    w_in = w_full[:3]
    w_out = w_full[3]
    rows_dev, trk_dev, width = fields.shape
    cell_count = rows_dev * lax.axis_size("grp") * trk_dev * lax.axis_size("trk")
    normed, centred, inv_std = normalize(fields, ln_gain)
    query_proj, key_proj, value_proj = project(normed, w_in)
    query_rows, key_rows, value_rows, upstream_rows = (
        lax.all_to_all(query_proj, "trk", split_axis=0, concat_axis=1, tiled=True),
        lax.all_to_all(key_proj, "trk", split_axis=0, concat_axis=1, tiled=True),
        lax.all_to_all(value_proj, "trk", split_axis=0, concat_axis=1, tiled=True),
        lax.all_to_all(upstream, "trk", split_axis=0, concat_axis=1, tiled=True),
    )
    attended, grad_query, grad_key, grad_value = attend_back(
        query_rows, key_rows, value_rows, upstream_rows, w_out
    )
    back_query, back_key, back_value = (
        lax.all_to_all(grad_query, "trk", split_axis=1, concat_axis=0, tiled=True),
        lax.all_to_all(grad_key, "trk", split_axis=1, concat_axis=0, tiled=True),
        lax.all_to_all(grad_value, "trk", split_axis=1, concat_axis=0, tiled=True),
    )
    grad_list = proj_grads(normed, back_query, back_key, back_value)
    branch_cells, gain_term = input_grad(
        back_query, back_key, back_value, w_in, centred, inv_std, ln_gain
    )
    out_grad = jnp.einsum(
        "rti,rtj->ij", attended, upstream_rows, preferred_element_type=jnp.float32
    )
    raw_grad = jnp.stack(grad_list + [out_grad])
    partial_grad = lax.psum_scatter(
        raw_grad.astype(jnp.bfloat16), "grp", scatter_dimension=1, tiled=True
    ).astype(jnp.float32)
    summed_grad = lax.psum_scatter(partial_grad, "trk", scatter_dimension=2, tiled=True)
    gain_sum = lax.psum(gain_term, ("grp", "trk"))
    factor = float(cell_count) ** (-0.5)
    grad_fields = (upstream.astype(jnp.float32) + branch_cells.astype(jnp.float32)).astype(
        jnp.bfloat16
    )
    return (grad_fields, summed_grad * factor, gain_sum * factor)


def solution(mesh):
    in_specs = (P("grp", "trk", None), P("grp", "trk", None), P(), P(None, "grp", "trk"))
    out_specs = (P("grp", "trk", None), P(None, "grp", "trk"), P())
    return jax.shard_map(shards, mesh=mesh, in_specs=in_specs, out_specs=out_specs, check_vma=False)
```

profile of v0, /device:TPU:2, one launch (start us, length us, event | category | flops | bytes accessed | tf_op | source)
XLA Modules:
  0.0 1188.6 jit_solution(13073194801549360445)
XLA Ops:
  8.0 184.0 %all_gather.6 = bf16[4,128,512]{1,0,2:T(4,128)(2,1)S(1)} all-gather(bf16[4,128,8]{1,0,2:T(4,128)(2,1)S(1)} %copy.57), channel_id=1, replica_groups=mesh['grp'=4,'trk'=64] {'trk'}, dimensions={2}, use_global_device_ids=true | all-gather | bytes 532480 | tf_op jit(solution)/shard_map/all_gather | solution.py:112
  193.1 8.9 all-to-all-start.3
  202.5 21.9 %all-gather.2.cloned.1.call-done = bf16[4,512,512]{2,1,0:T(8,128)(2,1)} async-done(((bf16[4,128,512]{2,1,0:T(8,128)(2,1)}), bf16[4,512,512]{2,1,0:T(8,128)(2,1)}) %all-gather.2.cloned.1.call-update) | async-done | bytes 2097168 | tf_op jit(solution)/shard_map/all_gather | solution.py:113
  224.3 2.3 convolution_convert_fusion.8
  226.6 13.0 %all-to-all-start = ((bf16[64,8,512]{2,1,0:T(8,128)(2,1)}), bf16[64,8,512]{2,1,0:T(8,128)(2,1)S(1)}, u32[]{:S(2)}, u32[]{:S(2)}) async-start(bf16[64,8,512]{2,1,0:T(8,128)(2,1)} %convolution_convert_fusion.8), calls=%async_computation | async-start | bytes 1048576 | tf_op jit(solution)/shard_map/all_to_all | solution.py:121
  239.7 2.3 convolution_convert_fusion.7
  242.0 16.4 %all-to-all-done = bf16[64,8,512]{2,1,0:T(8,128)(2,1)S(1)} async-done(((bf16[64,8,512]{2,1,0:T(8,128)(2,1)}), bf16[64,8,512]{2,1,0:T(8,128)(2,1)S(1)}, u32[]{:S(2)}, u32[]{:S(2)}) %all-to-all-start) | async-done | bytes 524320 | tf_op jit(solution)/shard_map/all_to_all | solution.py:121
  258.4 6.5 all-to-all-start.1
  265.0 2.3 convolution_convert_fusion.6
  267.3 15.6 %all-to-all-done.1 = bf16[64,8,512]{2,1,0:T(8,128)(2,1)S(1)} async-done(((bf16[64,8,512]{2,1,0:T(8,128)(2,1)}), bf16[64,8,512]{2,1,0:T(8,128)(2,1)S(1)}, u32[]{:S(2)}, u32[]{:S(2)}) %all-to-all-start.1) | async-done | bytes 524320 | tf_op jit(solution)/shard_map/all_to_all | solution.py:122
  282.9 6.7 all-to-all-start.2
  293.1 2.4 reshape.122
  296.9 9.8 all-to-all-done.2
  306.7 2.4 reshape.124
  309.1 2.3 copy.62
  311.4 60.7 %while.16 = (s32[]{:T(128)}, bf16[8,512,64]{1,2,0:T(8,128)(2,1)}, bf16[8,512,64]{1,2,0:T(8,128)(2,1)}, bf16[8,512,64]{1,2,0:T(8,128)(2,1)}, bf16[8,512,64]{1,2,0...) while((s32[]{:T(128)}, bf16[8,512,64]{1,2,0:T(8,128)(2,1)}, ...), condition=%wide.region_6.7_spmd, body=%wide.region_2.6_spmd.sunk | while | flops 206699008 | bytes 11305061 | solution.py:78
  311.9 1.8 fusion.112
  317.2 1.8 fusion.109
  319.5 1.8 fusion.112
  324.8 1.8 fusion.109
  327.1 1.8 fusion.112
  332.4 1.8 fusion.109
  334.7 1.8 fusion.112
  339.9 1.8 fusion.109
  342.3 1.8 fusion.112
  349.9 1.8 fusion.112
  357.5 1.8 fusion.112
  365.0 1.8 fusion.112
  372.1 2.4 copy.65
  375.1 3.8 reduce.1
  379.9 6.5 all-to-all-start.6
  386.4 2.4 copy.64
  388.8 3.8 reduce.2
  393.6 9.5 all-to-all-done.6
  403.1 6.7 all-to-all-start.5
  409.8 2.4 copy.63
  412.2 3.8 reduce.3
  417.1 2.3 fusion.55
  419.9 6.2 all-to-all-done.5
  426.1 6.6 all-to-all-start.4
  434.4 3.6 reshape.149
  439.5 8.9 all-to-all-done.4
  450.2 2.0 fusion.58
  458.0 21.6 %reduce-scatter.2.cloned.1.call-done = bf16[4,128,512]{2,1,0:T(8,128)(2,1)} async-done(((bf16[4,512,512]{2,1,0:T(8,128)(2,1)}), bf16[4,128,512]{2,1,0:T(8,128)(2,1)}) %reduce-scatter.2.cloned.1.call-update) | async-done | bytes 524304 | tf_op jit(solution)/shard_map/reduce_scatter | solution.py:142
  479.6 2.3 copy.69
  481.9 2.8 fusion.64
  484.8 76.2 %psum.7 = f32[512]{0:T(512)S(1)} all-reduce(f32[512]{0:T(512)S(1)} %get-tuple-element.108), channel_id=1, replica_groups=mesh['grp'=4,'trk'=64] {'grp','trk'}, use_global_device_ids=true, to_apply=%region_12.13 | all-reduce | flops 512 | bytes 4096 | tf_op jit(solution)/shard_map/psum | solution.py:146
  562.8 617.9 %all-reduce.3.cloned.1.call-done = f32[4,128,512]{1,0,2:T(4,128)} async-done(((f32[4,128,512]{1,0,2:T(4,128)}), f32[4,128,512]{1,0,2:T(4,128)}) %all-reduce.3.cloned.1.call-update) | async-done | bytes 1048592
  (112 shorter events, 63.0 us)
Async XLA Ops:
  7.2 194.8 %copy-start = (bf16[64,8,512]{2,1,0:T(8,128)(2,1)S(1)}, bf16[64,8,512]{2,1,0:T(8,128)(2,1)}, u32[]{:S(2)}) copy-start(bf16[64,8,512]{2,1,0:T(8,128)(2,1)} %param.6) | copy-start | bytes 1572868
  7.2 217.1 %all-gather.2.cloned.1.call-start = ((), (), s32[]{:S(2)}) async-start(), calls=%async_computation.8 | async-start | bytes 2621440 | tf_op jit(solution)/shard_map/all_gather | solution.py:113
  8.0 216.3 %copy-start.8 = (f32[512]{0:T(512)S(1)}, f32[512]{0:T(512)}, u32[]{:S(2)}) copy-start(f32[512]{0:T(512)} %param.8) | copy-start | bytes 6148
  193.1 33.6 %all-to-all-start.3 = ((bf16[64,8,512]{2,1,0:T(8,128)(2,1)}), bf16[64,8,512]{2,1,0:T(8,128)(2,1)S(1)}, u32[]{:S(2)}, u32[]{:S(2)}) async-start(bf16[64,8,512]{2,1,0:T(8,128)(2,1)} %param.7), calls=%async_computation.3 | async-start | bytes 1048576 | tf_op jit(solution)/shard_map/all_to_all | solution.py:124
  226.6 31.8 %all-to-all-start = ((bf16[64,8,512]{2,1,0:T(8,128)(2,1)}), bf16[64,8,512]{2,1,0:T(8,128)(2,1)S(1)}, u32[]{:S(2)}, u32[]{:S(2)}) async-start(bf16[64,8,512]{2,1,0:T(8,128)(2,1)} %convolution_convert_fusion.8), calls=%async_computation | async-start | bytes 1048576 | tf_op jit(solution)/shard_map/all_to_all | solution.py:121
  258.4 24.4 %all-to-all-start.1 = ((bf16[64,8,512]{2,1,0:T(8,128)(2,1)}), bf16[64,8,512]{2,1,0:T(8,128)(2,1)S(1)}, u32[]{:S(2)}, u32[]{:S(2)}) async-start(bf16[64,8,512]{2,1,0:T(8,128)(2,1)} %convolution_convert_fusion.7), calls=%async_computation.1 | async-start | bytes 1048576 | tf_op jit(solution)/shard_map/all_to_all | solution.py:122
  282.9 9.6 copy-start.2
  282.9 23.8 %all-to-all-start.2 = ((bf16[64,8,512]{2,1,0:T(8,128)(2,1)}), bf16[64,8,512]{2,1,0:T(8,128)(2,1)}, u32[]{:S(2)}, u32[]{:S(2)}) async-start(bf16[64,8,512]{2,1,0:T(8,128)(2,1)} %convolution_convert_fusion.6), calls=%async_computation.2 | async-start | bytes 1048576 | tf_op jit(solution)/shard_map/all_to_all | solution.py:123
  379.9 23.2 %all-to-all-start.6 = ((bf16[64,2,2048]{2,1,0:T(2,128)(2,1)}), bf16[64,2,2048]{2,1,0:T(2,128)(2,1)S(1)}, u32[]{:S(2)}, u32[]{:S(2)}) async-start(bf16[64,2,2048]{2,1,0:T(2,128)(2,1)} %reshape.146), calls=%async_computation.6 | async-start | bytes 1048576 | tf_op jit(solution)/shard_map/all_to_all | solution.py:132
  403.1 22.9 %all-to-all-start.5 = ((bf16[64,2,2048]{2,1,0:T(2,128)(2,1)}), bf16[64,2,2048]{2,1,0:T(2,128)(2,1)}, u32[]{:S(2)}, u32[]{:S(2)}) async-start(bf16[64,2,2048]{2,1,0:T(2,128)(2,1)} %reshape.148), calls=%async_computation.5 | async-start | bytes 1048576 | tf_op jit(solution)/shard_map/all_to_all | solution.py:131
  426.1 22.4 %all-to-all-start.4 = ((bf16[64,2,2048]{2,1,0:T(2,128)(2,1)}), bf16[64,2,2048]{2,1,0:T(2,128)(2,1)S(1)}, u32[]{:S(2)}, u32[]{:S(2)}) async-start(bf16[64,2,2048]{2,1,0:T(2,128)(2,1)} %reshape.150), calls=%async_computation.4 | async-start | bytes 1048576 | tf_op jit(solution)/shard_map/all_to_all | solution.py:130
  432.6 47.0 %reduce-scatter.2.cloned.1.call-start = ((), (), s32[]{:S(2)}) async-start(), calls=%async_computation.9 | async-start | bytes 2621440 | tf_op jit(solution)/shard_map/reduce_scatter | solution.py:142
  450.2 2.0 copy-start.4
  450.2 2.0 copy-start.6
  450.2 2.0 copy-start.7
  453.9 0.7 copy-start.9
  453.9 726.9 %all-reduce.3.cloned.1.call-start = ((), (), s32[]{:S(2)}) async-start(), calls=%async_computation.10 | async-start | bytes 2097152
  455.8 1.3 copy-start.1
  457.1 24.8 %copy-start.5 = (bf16[1,512,512]{2,1,0:T(8,128)(2,1)S(1)}, bf16[1,512,512]{2,1,0:T(8,128)(2,1)}, u32[]{:S(2)}) copy-start(bf16[1,512,512]{2,1,0:T(8,128)(2,1)} %copy.94) | copy-start | bytes 1572868
  481.9 79.7 %copy-start.3 = (bf16[64,8,512]{2,1,0:T(8,128)(2,1)S(1)}, bf16[64,8,512]{2,1,0:T(8,128)(2,1)}, u32[]{:S(2)}) copy-start(bf16[64,8,512]{2,1,0:T(8,128)(2,1)} %param.7) | copy-start | bytes 1572868
Sparse Core Ops, SparseCore 0:
  193.2 31.0 all-gather.1
  454.0 25.5 reduce-scatter.1
  482.4 698.3 all-reduce.2
where the time goes:
time: 1190 us
  waiting for transfers between devices  728 us (61%)
  blocking collectives  260 us (22%)
  matrix products  75.3 us (6%)
  starting transfers between devices  55.3 us (5%)
  local copies, waits for them, and re-layouts  35.4 us (3%)
  other arithmetic  19.9 us (2%)
  between operations  14.7 us (1%)
    unnamed x4, waiting for transfers between devices  618 us
    all_gather x1, blocking collectives, shards(): w_part = lax.all_gather(weights, 'trk', axis=2, tiled=True)  184 us
    psum x1, blocking collectives, shards(): gain_sum = lax.psum(gain_term, ('grp', 'trk'))  76.2 us
  transfers between devices with their start and end apart: 10, of which 9 were waited for; matrix products, arithmetic and copies ran while one was open for 4% of the time, Pallas kernels for 0%

commit v1 on v0

--- a/solution.py
+++ b/solution.py
@@ -143,7 +143,8 @@
         raw_grad.astype(jnp.bfloat16), "grp", scatter_dimension=1, tiled=True
     ).astype(jnp.float32)
     summed_grad = lax.psum_scatter(partial_grad, "trk", scatter_dimension=2, tiled=True)
-    gain_sum = lax.psum(gain_term, ("grp", "trk"))
+    one_axis = lax.psum(gain_term, "trk")
+    gain_sum = lax.psum(one_axis, "grp")
     factor = float(cell_count) ** (-0.5)
     grad_fields = (upstream.astype(jnp.float32) + branch_cells.astype(jnp.float32)).astype(
         jnp.bfloat16

time: 1190 us -> 1190 us (level)
  blocking collectives: 260 us -> 370 us
  waiting for transfers between devices: 728 us -> 618 us
    unnamed x4, waiting for transfers between devices: 618 us -> 509 us
    psum x1 -> x2, blocking collectives: 76.2 us -> 186 us  [the longest x1 180 us: shards(): one_axis = lax.psum(gain_term, 'trk')]
where the time goes in v1:
time: 1190 us
  waiting for transfers between devices  618 us (52%)
  blocking collectives  370 us (31%)
  matrix products  75.3 us (6%)
  starting transfers between devices  56.8 us (5%)
  local copies, waits for them, and re-layouts  35.4 us (3%)
  other arithmetic  20.7 us (2%)
  between operations  14.7 us (1%)
    unnamed x4, waiting for transfers between devices  509 us
    all_gather x1, blocking collectives, shards(): w_part = lax.all_gather(weights, 'trk', axis=2, tiled=True)  184 us
    psum x1, blocking collectives, shards(): one_axis = lax.psum(gain_term, 'trk')  180 us
  transfers between devices with their start and end apart: 10, of which 9 were waited for; matrix products, arithmetic and copies ran while one was open for 4% of the time, Pallas kernels for 0%

profile of v1, /device:TPU:2, one launch (start us, length us, event | category | flops | bytes accessed | tf_op | source)
XLA Modules:
  0.0 1190.2 jit_solution(13712254902822985866)
XLA Ops:
  8.0 184.0 %all_gather.6 = bf16[4,128,512]{1,0,2:T(4,128)(2,1)S(1)} all-gather(bf16[4,128,8]{1,0,2:T(4,128)(2,1)S(1)} %copy.57), channel_id=1, replica_groups=mesh['grp'=4,'trk'=64] {'trk'}, dimensions={2}, use_global_device_ids=true | all-gather | bytes 532480 | tf_op jit(solution)/shard_map/all_gather | solution.py:112
  193.1 8.9 all-to-all-start.3
  202.5 21.9 %all-gather.2.cloned.1.call-done = bf16[4,512,512]{2,1,0:T(8,128)(2,1)} async-done(((bf16[4,128,512]{2,1,0:T(8,128)(2,1)}), bf16[4,512,512]{2,1,0:T(8,128)(2,1)}) %all-gather.2.cloned.1.call-update) | async-done | bytes 2097168 | tf_op jit(solution)/shard_map/all_gather | solution.py:113
  224.3 2.3 convolution_convert_fusion.8
  226.6 13.0 %all-to-all-start = ((bf16[64,8,512]{2,1,0:T(8,128)(2,1)}), bf16[64,8,512]{2,1,0:T(8,128)(2,1)S(1)}, u32[]{:S(2)}, u32[]{:S(2)}) async-start(bf16[64,8,512]{2,1,0:T(8,128)(2,1)} %convolution_convert_fusion.8), calls=%async_computation | async-start | bytes 1048576 | tf_op jit(solution)/shard_map/all_to_all | solution.py:121
  239.7 2.3 convolution_convert_fusion.7
  242.0 16.4 %all-to-all-done = bf16[64,8,512]{2,1,0:T(8,128)(2,1)S(1)} async-done(((bf16[64,8,512]{2,1,0:T(8,128)(2,1)}), bf16[64,8,512]{2,1,0:T(8,128)(2,1)S(1)}, u32[]{:S(2)}, u32[]{:S(2)}) %all-to-all-start) | async-done | bytes 524320 | tf_op jit(solution)/shard_map/all_to_all | solution.py:121
  258.4 6.5 all-to-all-start.1
  265.0 2.3 convolution_convert_fusion.6
  267.3 15.6 %all-to-all-done.1 = bf16[64,8,512]{2,1,0:T(8,128)(2,1)S(1)} async-done(((bf16[64,8,512]{2,1,0:T(8,128)(2,1)}), bf16[64,8,512]{2,1,0:T(8,128)(2,1)S(1)}, u32[]{:S(2)}, u32[]{:S(2)}) %all-to-all-start.1) | async-done | bytes 524320 | tf_op jit(solution)/shard_map/all_to_all | solution.py:122
  282.8 6.7 all-to-all-start.2
  293.1 2.4 reshape.122
  296.9 9.8 all-to-all-done.2
  306.7 2.4 reshape.124
  309.1 2.3 copy.62
  311.4 60.7 %while.16 = (s32[]{:T(128)}, bf16[8,512,64]{1,2,0:T(8,128)(2,1)}, bf16[8,512,64]{1,2,0:T(8,128)(2,1)}, bf16[8,512,64]{1,2,0:T(8,128)(2,1)}, bf16[8,512,64]{1,2,0...) while((s32[]{:T(128)}, bf16[8,512,64]{1,2,0:T(8,128)(2,1)}, ...), condition=%wide.region_6.7_spmd, body=%wide.region_2.6_spmd.sunk | while | flops 206699008 | bytes 11305061 | solution.py:78
  311.9 1.8 fusion.112
  317.2 1.8 fusion.109
  319.5 1.8 fusion.112
  324.8 1.8 fusion.109
  327.1 1.8 fusion.112
  332.3 1.8 fusion.109
  334.7 1.8 fusion.112
  342.3 1.8 fusion.112
  349.9 1.8 fusion.112
  357.4 1.8 fusion.112
  365.0 1.8 fusion.112
  372.1 2.4 copy.65
  375.1 3.8 reduce.1
  379.9 6.5 all-to-all-start.6
  387.3 3.8 reduce.2
  392.1 11.0 all-to-all-done.6
  403.1 6.5 all-to-all-start.5
  409.6 2.4 copy.63
  412.0 4.6 reduce.3
  416.7 2.0 reshape.150
  418.7 2.3 fusion.55
  421.5 4.5 all-to-all-done.5
  426.0 8.3 all-to-all-start.4
  436.0 3.6 reshape.149
  441.2 8.9 all-to-all-done.4
  451.8 2.0 fusion.58
  460.1 21.1 %reduce-scatter.2.cloned.1.call-done = bf16[4,128,512]{2,1,0:T(8,128)(2,1)} async-done(((bf16[4,512,512]{2,1,0:T(8,128)(2,1)}), bf16[4,128,512]{2,1,0:T(8,128)(2,1)}) %reduce-scatter.2.cloned.1.call-update) | async-done | bytes 524304 | tf_op jit(solution)/shard_map/reduce_scatter | solution.py:142
  481.2 2.3 copy.69
  483.5 2.8 fusion.64
  486.3 179.9 %psum.14 = f32[512]{0:T(512)S(1)} all-reduce(f32[512]{0:T(512)S(1)} %get-tuple-element.108), channel_id=1, replica_groups=mesh['grp'=4,'trk'=64] {'trk'}, use_global_device_ids=true, to_apply=%region_12.13 | all-reduce | flops 512 | bytes 4096 | tf_op jit(solution)/shard_map/psum | solution.py:146
  666.2 5.7 psum.15
  673.8 508.5 %all-reduce.3.cloned.1.call-done = f32[4,128,512]{1,0,2:T(4,128)} async-done(((f32[4,128,512]{1,0,2:T(4,128)}), f32[4,128,512]{1,0,2:T(4,128)}) %all-reduce.3.cloned.1.call-update) | async-done | bytes 1048592
  (119 shorter events, 65.3 us)
Async XLA Ops:
  7.2 194.8 %copy-start = (bf16[64,8,512]{2,1,0:T(8,128)(2,1)S(1)}, bf16[64,8,512]{2,1,0:T(8,128)(2,1)}, u32[]{:S(2)}) copy-start(bf16[64,8,512]{2,1,0:T(8,128)(2,1)} %param.6) | copy-start | bytes 1572868
  7.2 217.1 %all-gather.2.cloned.1.call-start = ((), (), s32[]{:S(2)}) async-start(), calls=%async_computation.8 | async-start | bytes 2621440 | tf_op jit(solution)/shard_map/all_gather | solution.py:113
  8.0 216.3 %copy-start.11 = (f32[512]{0:T(512)S(1)}, f32[512]{0:T(512)}, u32[]{:S(2)}) copy-start(f32[512]{0:T(512)} %param.8) | copy-start | bytes 6148
  193.1 33.6 %all-to-all-start.3 = ((bf16[64,8,512]{2,1,0:T(8,128)(2,1)}), bf16[64,8,512]{2,1,0:T(8,128)(2,1)S(1)}, u32[]{:S(2)}, u32[]{:S(2)}) async-start(bf16[64,8,512]{2,1,0:T(8,128)(2,1)} %param.7), calls=%async_computation.3 | async-start | bytes 1048576 | tf_op jit(solution)/shard_map/all_to_all | solution.py:124
  226.6 31.8 %all-to-all-start = ((bf16[64,8,512]{2,1,0:T(8,128)(2,1)}), bf16[64,8,512]{2,1,0:T(8,128)(2,1)S(1)}, u32[]{:S(2)}, u32[]{:S(2)}) async-start(bf16[64,8,512]{2,1,0:T(8,128)(2,1)} %convolution_convert_fusion.8), calls=%async_computation | async-start | bytes 1048576 | tf_op jit(solution)/shard_map/all_to_all | solution.py:121
  258.4 24.4 %all-to-all-start.1 = ((bf16[64,8,512]{2,1,0:T(8,128)(2,1)}), bf16[64,8,512]{2,1,0:T(8,128)(2,1)S(1)}, u32[]{:S(2)}, u32[]{:S(2)}) async-start(bf16[64,8,512]{2,1,0:T(8,128)(2,1)} %convolution_convert_fusion.7), calls=%async_computation.1 | async-start | bytes 1048576 | tf_op jit(solution)/shard_map/all_to_all | solution.py:122
  282.8 9.6 copy-start.3
  282.8 23.8 %all-to-all-start.2 = ((bf16[64,8,512]{2,1,0:T(8,128)(2,1)}), bf16[64,8,512]{2,1,0:T(8,128)(2,1)}, u32[]{:S(2)}, u32[]{:S(2)}) async-start(bf16[64,8,512]{2,1,0:T(8,128)(2,1)} %convolution_convert_fusion.6), calls=%async_computation.2 | async-start | bytes 1048576 | tf_op jit(solution)/shard_map/all_to_all | solution.py:123
  374.5 11.9 copy-start.6
  379.9 23.2 %all-to-all-start.6 = ((bf16[64,2,2048]{2,1,0:T(2,128)(2,1)}), bf16[64,2,2048]{2,1,0:T(2,128)(2,1)S(1)}, u32[]{:S(2)}, u32[]{:S(2)}) async-start(bf16[64,2,2048]{2,1,0:T(2,128)(2,1)} %reshape.146), calls=%async_computation.6 | async-start | bytes 1048576 | tf_op jit(solution)/shard_map/all_to_all | solution.py:132
  403.1 22.8 %all-to-all-start.5 = ((bf16[64,2,2048]{2,1,0:T(2,128)(2,1)}), bf16[64,2,2048]{2,1,0:T(2,128)(2,1)S(1)}, u32[]{:S(2)}, u32[]{:S(2)}) async-start(bf16[64,2,2048]{2,1,0:T(2,128)(2,1)} %reshape.148), calls=%async_computation.5 | async-start | bytes 1048576 | tf_op jit(solution)/shard_map/all_to_all | solution.py:131
  426.0 8.6 copy-start.2
  426.0 24.0 %all-to-all-start.4 = ((bf16[64,2,2048]{2,1,0:T(2,128)(2,1)}), bf16[64,2,2048]{2,1,0:T(2,128)(2,1)S(1)}, u32[]{:S(2)}, u32[]{:S(2)}) async-start(bf16[64,2,2048]{2,1,0:T(2,128)(2,1)} %reshape.150), calls=%async_computation.4 | async-start | bytes 1048576 | tf_op jit(solution)/shard_map/all_to_all | solution.py:130
  434.3 46.9 %reduce-scatter.2.cloned.1.call-start = ((), (), s32[]{:S(2)}) async-start(), calls=%async_computation.9 | async-start | bytes 2621440 | tf_op jit(solution)/shard_map/reduce_scatter | solution.py:142
  451.8 2.0 copy-start.5
  451.8 2.0 copy-start.9
  451.8 2.0 copy-start.10
  455.4 0.7 copy-start.12
  455.5 726.9 %all-reduce.3.cloned.1.call-start = ((), (), s32[]{:S(2)}) async-start(), calls=%async_computation.10 | async-start | bytes 2097152
  457.3 1.9 copy-start.1
  459.2 24.3 %copy-start.7 = (bf16[1,512,512]{2,1,0:T(8,128)(2,1)S(1)}, bf16[1,512,512]{2,1,0:T(8,128)(2,1)}, u32[]{:S(2)}) copy-start(bf16[1,512,512]{2,1,0:T(8,128)(2,1)} %copy.93) | copy-start | bytes 1572868
  459.2 24.3 %copy-start.8 = (bf16[1,512,512]{2,1,0:T(8,128)(2,1)S(1)}, bf16[1,512,512]{2,1,0:T(8,128)(2,1)}, u32[]{:S(2)}) copy-start(bf16[1,512,512]{2,1,0:T(8,128)(2,1)} %copy.94) | copy-start | bytes 1572868
  483.5 189.1 %copy-start.4 = (bf16[64,8,512]{2,1,0:T(8,128)(2,1)S(1)}, bf16[64,8,512]{2,1,0:T(8,128)(2,1)}, u32[]{:S(2)}) copy-start(bf16[64,8,512]{2,1,0:T(8,128)(2,1)} %param.7) | copy-start | bytes 1572868
Sparse Core Ops, SparseCore 0:
  193.2 31.0 all-gather.1
  455.6 25.5 reduce-scatter.1
  484.0 698.3 all-reduce.2
